TPU v7x, 32 devices: a whole 2x2x4 slice. The times are simulated.
32 devices in a mesh: prow: 4 (over z), pcol: 8 (over y, x, core).
Axes of the slice: x: 2, y: 2, z: 4, core: 2. Of those that a mesh axis runs over, the one named last changes fastest.
Arguments:
- site_code: int32 [17408], P(('prow', 'pcol')), may hold values from 0 to 285212671, as said below
- length_scale: float32 [1], replicated, may hold values from 6 to 12
- noise_var: float32 [1], replicated, may hold values from 0.3 to 1
Outputs:
- panel: bfloat16 [16, 1024, 1024], P('prow')
- trailing: bfloat16 [16, 1024, 8, 1024], P('prow', None, 'pcol')
Inputs may be any that keep to these rules, and one draw needn't show every extreme that they name: `site_code`: each entry is 128 * 128 * s + 128 * x + y for a slot s and bins x, y in 0 .. 127; every slot of 0 .. 17407 appears once. With b = s // 1024 and r = s mod 1024, the home of slot s is the device of prow-major index r mod (32) if b = 0, else the device (prow (b - 1) mod 4, pcol r mod 8); no device holds more than 17 sites of one home, and some device holds exactly 17 sites of some home.
All inputs are finite; a program needn't handle non-finite values.
Results may differ from a plain program's by a relative error of at most 0.0036.
Values may be sent and summed in bfloat16 or wider, within the bound.
No kernel may reach another device: no remote copies, remote signals or barrier semaphores. Data moves between devices by JAX's collectives and lax.ppermute only.
A program may use at most 192 MiB of HBM per device.

v0:
```python
import jax
import jax.numpy as jnp
from jax import lax
from jax.sharding import PartitionSpec as P

B = 1024
GRID = 128
TR_DEV = 4
SLAB_DEV = 1


def from_root(value, axis, source):
    kept = jnp.where(lax.axis_index(axis) == source, value, 0).astype(value.dtype)
    return lax.psum(kept, axis)


def site_features(codes):
    coord_x = (codes // GRID % GRID).astype(jnp.float32)
    coord_y = (codes % GRID).astype(jnp.float32)
    radius_sq = coord_x * coord_x + coord_y * coord_y
    ones = jnp.ones_like(coord_x)
    left = jnp.stack([coord_x, coord_y, radius_sq, ones], -2)
    right = jnp.stack([-2.0 * coord_x, -2.0 * coord_y, ones, radius_sq], -2)
    return (left, right)


def cov_tile(left, right, decay_rate, nugget, same):
    squared = jnp.einsum("...ka,kb->...ab", left, right, precision=lax.Precision.HIGHEST)
    distance = jnp.sqrt(jnp.maximum(squared, 0.0))
    scaled = decay_rate * distance
    values = (1.0 + scaled) * jnp.exp(-scaled)
    rank_count = values.ndim
    eye_mask = lax.broadcasted_iota(
        jnp.int32, values.shape, rank_count - 2
    ) == lax.broadcasted_iota(jnp.int32, values.shape, rank_count - 1)
    return values + jnp.where(eye_mask, nugget * same, 0.0)


def body(site_code, length_scale, noise_var):
    n_prow = lax.axis_size("prow")
    n_pcol = lax.axis_size("pcol")
    devices = n_prow * n_pcol
    me_row = lax.axis_index("prow")
    me_col = lax.axis_index("pcol")
    decay_rate = jnp.sqrt(3.0) / length_scale[0]
    nugget = noise_var[0]
    pick_index = me_col // n_prow + jnp.arange(SLAB_DEV, dtype=jnp.int32) * (n_pcol // n_prow)
    capacity = (TR_DEV * B // n_pcol + B // devices + devices - 1) // devices
    site_slot = site_code // (GRID * GRID)
    block_id = site_slot // B
    block_pos = site_slot % B
    home_dev = jnp.where(
        block_id == 0, block_pos % devices, (block_id - 1) % n_prow * n_pcol + block_pos % n_pcol
    )
    one_hot = (home_dev[:, None] == jnp.arange(devices, dtype=jnp.int32)[None, :]).astype(jnp.int32)
    arrival_rank = jnp.sum(jnp.cumsum(one_hot, axis=0) * one_hot, axis=1) - 1
    outbox = jnp.full((devices, capacity), -1, jnp.int32).at[home_dev, arrival_rank].set(site_code)
    inbox = lax.all_to_all(
        outbox, ("prow", "pcol"), split_axis=0, concat_axis=0, tiled=True
    ).reshape(-1)
    valid = inbox >= 0
    got_slot = jnp.where(valid, inbox // (GRID * GRID), 0)
    got_block = got_slot // B
    got_pos = got_slot % B
    row_width = B // n_pcol
    tile_index = jnp.where(valid & (got_block > 0), (got_block - 1) // n_prow, TR_DEV)
    row_home = (
        jnp.full((TR_DEV, row_width), -1, jnp.int32)
        .at[tile_index, got_pos // n_pcol]
        .set(inbox, mode="drop")
    )
    panel_width = B // devices
    panel_index = jnp.where(valid & (got_block == 0), got_pos // devices, panel_width)
    panel_home = jnp.full((panel_width,), -1, jnp.int32).at[panel_index].set(inbox, mode="drop")
    row_all = lax.all_gather(row_home, "pcol", axis=1, tiled=True)
    row_codes = row_all.reshape(TR_DEV, n_pcol, row_width).transpose(0, 2, 1).reshape(TR_DEV, B)
    panel_all = lax.all_gather(panel_home, ("prow", "pcol"), axis=0, tiled=True)
    panel_codes = panel_all.reshape(devices, panel_width).T.reshape(B)
    col_codes = from_root(jnp.take(row_codes, pick_index, axis=0), "prow", me_col % n_prow)
    panel_left, panel_right = site_features(panel_codes)
    row_left, row_right = site_features(row_codes)
    col_left, col_right = site_features(col_codes)

    def factor_panel(unused):
        diag_factor = jnp.linalg.cholesky(
            cov_tile(panel_left, panel_right, decay_rate, nugget, 1.0)
        )
        tiles = cov_tile(row_left, panel_right, decay_rate, nugget, 0.0)
        solved = jax.scipy.linalg.solve_triangular(
            diag_factor, tiles.reshape(TR_DEV * B, B).T, lower=True
        )
        return solved.T.reshape(TR_DEV, B, B).astype(jnp.bfloat16)

    def skip_panel(unused):
        return jnp.zeros((TR_DEV, B, B), jnp.bfloat16)

    panel_mine = lax.cond(me_col == 0, factor_panel, skip_panel, 0)
    panel_rows = from_root(panel_mine, "pcol", 0)
    panel_pick = jnp.take(panel_rows, pick_index, axis=0)
    panel_cols = from_root(panel_pick, "prow", me_col % n_prow)
    row_results = []
    for row_tile in range(TR_DEV):
        trail = row_tile * n_prow + me_row
        other = 0 + me_col
        same = jnp.where(trail == other, 1.0, 0.0)
        tile = cov_tile(row_left[row_tile], col_right[0], decay_rate, nugget, same)
        product = lax.dot_general(
            panel_rows[row_tile],
            panel_cols[0],
            (((1,), (1,)), ((), ())),
            preferred_element_type=jnp.float32,
        )
        col_results = [(tile - product).astype(jnp.bfloat16)]
        row_results.append(jnp.stack(col_results, 1))
    trailing = jnp.stack(row_results, 0)
    return (panel_rows, trailing)


def solution(mesh):
    in_specs = (P(("prow", "pcol")), P(), P())
    out_specs = (P("prow", None, None), P("prow", None, "pcol", None))
    return jax.shard_map(body, mesh=mesh, in_specs=in_specs, out_specs=out_specs, check_vma=False)
```

profile of v0, /device:TPU:0, one launch (start us, length us, event | category | flops | bytes accessed | tf_op | source)
XLA Modules:
  0.0 914.7 jit_solution(17226715184799600394)
XLA Ops:
  9.8 46.5 %scatter_fusion = s32[32,17]{0,1:T(8,128)S(1)} fusion(s32[32,17]{0,1:T(8,128)S(1)} %broadcast_in_dim.85, s32[544]{0:T(1024)S(1)} %fusion.113, s32[544]{0:T(1024)} %param.5), kind=kCustom, calls=%fused_computation | custom fusion | bytes 10880 | tf_op jit(solution)/shard_map/scatter | solution.py:57
  73.1 25.6 %scatter_fusion.1 = s32[4,128]{1,0:T(4,128)S(1)} fusion(s32[4,128]{1,0:T(4,128)S(1)} %broadcast_in_dim.87, s32[544]{0:T(1024)S(1)} %get-tuple-element.66, s32[544]{0:T(1024)S(1)} %reshape.975), kind=kCustom, calls=%fused_computation.2 | custom fusion | bytes 10880 | tf_op jit(solution)/shard_map/scatter | solution.py:70
  98.7 8.0 all_gather.7
  111.4 38.2 %all-reduce.2 = s32[1024]{0:T(1024)S(1)} all-reduce(s32[1024]{0:T(1024)S(1)} %dynamic-update-slice.49), channel_id=1, replica_groups=mesh['prow'=4,'pcol'=8] {'prow','pcol'}, use_global_device_ids=true, to_apply=%add.2 | all-reduce | flops 1024 | bytes 8192
  150.1 487.0 %conditional.1 = (bf16[4,1024,1024]{2,1,0:T(8,128)(2,1)}) conditional(s32[]{:T(128)} %convert_element_type.98, () %tuple.14, (f32[]{:T(128)}, f32[4,1024]{1,0:T(4,128)S(1)}, f32[4,1024]{1,0:T(4,128)S(1)}, f32[]{:T(128)}, f32[4,4,1024]{2,0,1:T(4,128)S(1)}) %tuple.15), branch_computations={%region_6.7_spmd, %region_7.24_spmd} | conditional | flops 32137316352 | bytes 414441856 | solution.py:97
  173.7 11.7 %cholesky.5 = f32[128,128]{1,0:T(8,128)S(1)} custom-call(f32[128,128]{1,0:T(8,128)S(1)} %cholesky.221), custom_call_target="Cholesky" | custom-call | tf_op jit(solution)/shard_map/cond/branch_1_fun/jit(cholesky)/cholesky | solution.py:85
  185.5 9.8 %custom-call.55 = f32[1,128,128]{1,2,0:T(8,128)S(1)} custom-call(f32[1,128,128]{2,1,0:T(8,128)S(1)} %get-tuple-element.130), custom_call_target="InvertDiagBlocksLowerTriangular" | custom-call | tf_op jit(solution)/shard_map/cond/branch_1_fun/jit(cholesky)/cholesky | solution.py:85
  201.7 11.9 %cholesky.27 = f32[128,128]{1,0:T(8,128)S(1)} custom-call(f32[128,128]{1,0:T(8,128)S(1)} %cholesky.227), custom_call_target="Cholesky" | custom-call | tf_op jit(solution)/shard_map/cond/branch_1_fun/jit(cholesky)/cholesky | solution.py:85
  216.2 9.8 %custom-call.56 = f32[1,128,128]{1,2,0:T(8,128)S(1)} custom-call(f32[1,128,128]{2,1,0:T(8,128)S(1)} %get-tuple-element.127), custom_call_target="InvertDiagBlocksLowerTriangular" | custom-call | tf_op jit(solution)/shard_map/cond/branch_1_fun/jit(cholesky)/cholesky | solution.py:85
  229.4 11.7 %cholesky.58 = f32[128,128]{1,0:T(8,128)S(1)} custom-call(f32[128,128]{1,0:T(8,128)S(1)} %cholesky.232), custom_call_target="Cholesky" | custom-call | tf_op jit(solution)/shard_map/cond/branch_1_fun/jit(cholesky)/cholesky | solution.py:85
  243.1 9.8 %custom-call.57 = f32[1,128,128]{1,2,0:T(8,128)S(1)} custom-call(f32[1,128,128]{2,1,0:T(8,128)S(1)} %get-tuple-element.124), custom_call_target="InvertDiagBlocksLowerTriangular" | custom-call | tf_op jit(solution)/shard_map/cond/branch_1_fun/jit(cholesky)/cholesky | solution.py:85
  256.9 11.7 %cholesky.87 = f32[128,128]{1,0:T(8,128)S(1)} custom-call(f32[128,128]{1,0:T(8,128)S(1)} %cholesky.237), custom_call_target="Cholesky" | custom-call | tf_op jit(solution)/shard_map/cond/branch_1_fun/jit(cholesky)/cholesky | solution.py:85
  270.6 9.8 %custom-call.58 = f32[1,128,128]{1,2,0:T(8,128)S(1)} custom-call(f32[1,128,128]{2,1,0:T(8,128)S(1)} %get-tuple-element.121), custom_call_target="InvertDiagBlocksLowerTriangular" | custom-call | tf_op jit(solution)/shard_map/cond/branch_1_fun/jit(cholesky)/cholesky | solution.py:85
  283.9 11.7 %cholesky.116 = f32[128,128]{1,0:T(8,128)S(1)} custom-call(f32[128,128]{1,0:T(8,128)S(1)} %cholesky.242), custom_call_target="Cholesky" | custom-call | tf_op jit(solution)/shard_map/cond/branch_1_fun/jit(cholesky)/cholesky | solution.py:85
  297.6 10.0 %custom-call.59 = f32[1,128,128]{1,2,0:T(8,128)S(1)} custom-call(f32[1,128,128]{2,1,0:T(8,128)S(1)} %get-tuple-element.118), custom_call_target="InvertDiagBlocksLowerTriangular" | custom-call | tf_op jit(solution)/shard_map/cond/branch_1_fun/jit(cholesky)/cholesky | solution.py:85
  310.9 11.7 %cholesky.146 = f32[128,128]{1,0:T(8,128)S(1)} custom-call(f32[128,128]{1,0:T(8,128)S(1)} %cholesky.249), custom_call_target="Cholesky" | custom-call | tf_op jit(solution)/shard_map/cond/branch_1_fun/jit(cholesky)/cholesky | solution.py:85
  324.7 9.8 %custom-call.60 = f32[1,128,128]{1,2,0:T(8,128)S(1)} custom-call(f32[1,128,128]{2,1,0:T(8,128)S(1)} %get-tuple-element.115), custom_call_target="InvertDiagBlocksLowerTriangular" | custom-call | tf_op jit(solution)/shard_map/cond/branch_1_fun/jit(cholesky)/cholesky | solution.py:85
  337.4 12.1 %cholesky.176 = f32[128,128]{1,0:T(8,128)S(1)} custom-call(f32[128,128]{1,0:T(8,128)S(1)} %cholesky.256), custom_call_target="Cholesky" | custom-call | tf_op jit(solution)/shard_map/cond/branch_1_fun/jit(cholesky)/cholesky | solution.py:85
  351.6 9.8 %custom-call.61 = f32[1,128,128]{1,2,0:T(8,128)S(1)} custom-call(f32[1,128,128]{2,1,0:T(8,128)S(1)} %get-tuple-element.112), custom_call_target="InvertDiagBlocksLowerTriangular" | custom-call | tf_op jit(solution)/shard_map/cond/branch_1_fun/jit(cholesky)/cholesky | solution.py:85
  364.0 11.7 %cholesky.204 = f32[128,128]{1,0:T(8,128)S(1)} custom-call(f32[128,128]{1,0:T(8,128)S(1)} %convolution_subtract_fusion.11), custom_call_target="Cholesky" | custom-call | tf_op jit(solution)/shard_map/cond/branch_1_fun/jit(cholesky)/cholesky | solution.py:85
  382.6 24.1 %while.3 = (s32[]{:T(128)}, f32[1024,1024]{1,0:T(8,128)}, s32[8,2]{0,1:T(2,128)S(1)}, f32[8,128,128]{2,1,0:T(8,128)S(1)}, s32[]{:T(128)}) while((s32[]{:T(128)}, f32[1024,1024]{1,0:T(8,128)}, s32[8,2]{0,1:T(2,128)S(1)}, f32[8,128,128]{2,1,0:T(8,128)S(1)}, s32[]{:T(128)}) %tuple.95), condition=%wide.while_cond, body=%wide.while_body.sunk | while | flops 2 | bytes 131189 | solution.py:89
  406.7 78.6 %custom-call.62 = f32[8,128,128]{1,2,0:T(8,128)S(1)} custom-call(f32[8,128,128]{2,1,0:T(8,128)S(1)} %get-tuple-element.27), custom_call_target="InvertDiagBlocksLowerTriangular" | custom-call | tf_op jit(solution)/shard_map/cond/branch_1_fun/jit(_solve_triangular)/triangular_solve | solution.py:89
  485.3 23.3 %select_add_fusion = f32[4,1024,1024]{2,1,0:T(8,128)} fusion(f32[]{:T(128)S(6)} %mul.122, f32[]{:T(128)} %get-tuple-element.4, f32[4,4,1024]{2,0,1:T(4,128)S(1)} %get-tuple-element.64, f32[4,1024]{1,0:T(4,128)S(1)} %get-tuple-element.15), kind=kOutput, calls=%fused_computation.5 | convolution fusion | flops 234881024 | bytes 16859144 | tf_op jit(solution)/shard_map/cond/branch_1_fun/...ka,kb->...ab/dot_general | solution.py:28
  508.6 17.6 %copy.28 = f32[4096,1024]{0,1:T(8,128)} copy(f32[4096,1024]{1,0:T(8,128)} %bitcast.202) | data formatting | bytes 33554432 | tf_op jit(solution)/shard_map/cond/branch_1_fun/reshape | solution.py:90
  581.3 9.3 %convolution_subtract_fusion.1 = f32[128,4096]{1,0:T(8,128)S(1)} fusion(f32[640,4096]{1,0:T(8,128)} %get-tuple-element.96, f32[1024,4096]{1,0:T(8,128)S(1)} %bitcast.199, f32[1024,1024]{1,0:T(8,128)} %get-tuple-element.212), kind=kOutput, calls=%fused_computation.22 | convolution fusion | flops 4027056128 | bytes 15007744 | tf_op jit(solution)/shard_map/cond/branch_1_fun/jit(_solve_triangular)/triangular_solve | solution.py:89
  596.0 9.8 %convolution_subtract_fusion = f32[128,4096]{1,0:T(8,128)S(1)} fusion(f32[768,4096]{1,0:T(8,128)} %get-tuple-element.93, f32[1024,4096]{1,0:T(8,128)S(1)} %bitcast.200, f32[1024,1024]{1,0:T(8,128)} %get-tuple-element.212), kind=kOutput, calls=%fused_computation.21 | convolution fusion | flops 4832362496 | bytes 17170432 | tf_op jit(solution)/shard_map/cond/branch_1_fun/jit(_solve_triangular)/triangular_solve | solution.py:89
  610.3 11.7 %convolution_subtract_fusion.4 = f32[128,4096]{1,0:T(8,128)S(1)} fusion(f32[896,4096]{1,0:T(8,128)} %constant_dynamic-update-slice_fusion.11, f32[1024,4096]{1,0:T(8,128)S(1)} %bitcast.201, f32[1024,1024]{1,0:T(8,128)} %get-tuple-element.212), kind=kOutput, calls=%fused_computation.25 | convolution fusion | flops 5637668864 | bytes 19333120 | tf_op jit(solution)/shard_map/cond/branch_1_fun/jit(_solve_triangular)/triangular_solve | solution.py:89
  624.9 11.9 %copy.38 = bf16[4096,1024]{1,0:T(8,128)(2,1)} copy(bf16[4096,1024]{0,1:T(8,128)(2,1)} %bitcast.26) | data formatting | bytes 16777216 | tf_op jit(solution)/shard_map/cond | solution.py:97
  644.5 123.6 %all-reduce.6.cloned.1.call-done = bf16[4,1024,1024]{2,1,0:T(8,128)(2,1)} async-done(((bf16[4,1024,1024]{2,1,0:T(8,128)(2,1)}), bf16[4,1024,1024]{2,1,0:T(8,128)(2,1)}) %all-reduce.6.cloned.1.call-update) | async-done | bytes 8388624 | tf_op jit(solution)/shard_map/psum | solution.py:14
  772.2 8.4 psum.22
  780.7 76.9 %all-reduce.8.cloned.1.call-done = bf16[1024,1024]{1,0:T(8,128)(2,1)} async-done(((bf16[1024,1024]{1,0:T(8,128)(2,1)}), bf16[1024,1024]{1,0:T(8,128)(2,1)}) %all-reduce.8.cloned.1.call-update) | async-done | bytes 2097168 | tf_op jit(solution)/shard_map/psum | solution.py:14
  899.7 7.8 copy.122
  (161 shorter events, 231.4 us)
Async XLA Ops:
  57.1 14.4 %all-to-all-start = ((s32[32,1,17]{2,1,0:T(1,128)}), s32[32,1,17]{2,1,0:T(1,128)S(1)}, u32[]{:S(2)}, u32[]{:S(2)}) async-start(s32[32,1,17]{2,1,0:T(1,128)} %copy.31), calls=%async_computation | async-start | bytes 32768 | tf_op jit(solution)/shard_map/all_to_all | solution.py:58
  64.4 703.7 %all-reduce.6.cloned.1.call-start = ((), (), s32[]{:S(2)}) async-start(), calls=%async_computation.1 | async-start | bytes 16777216 | tf_op jit(solution)/shard_map/psum | solution.py:14
  154.3 1.9 copy-start.1
  171.7 2.0 copy-start.2
  526.3 11.9 %copy-start = (f32[4096,1024]{0,1:T(8,128)S(1)}, f32[4096,1024]{0,1:T(8,128)}, u32[]{:S(2)}) copy-start(f32[4096,1024]{0,1:T(8,128)} %copy.28) | copy-start | bytes 50331652 | tf_op jit(solution)/shard_map/cond
  644.4 213.2 %all-reduce.8.cloned.1.call-start = ((), (), s32[]{:S(2)}) async-start(), calls=%async_computation.2 | async-start | bytes 4194304 | tf_op jit(solution)/shard_map/psum | solution.py:14
  862.2 6.1 copy-start.3
  862.2 16.3 %slice-start = ((s8[8388608]{0:T(1024)(128)(4,1)}), s8[4194304]{0:T(1024)(128)(4,1)S(1)}, s32[]{:S(2)}) async-start(s8[8388608]{0:T(1024)(128)(4,1)} %bitcast.203), calls=%async_computation.3 | async-start | bytes 8388608
  868.3 10.2 %slice-start.1 = ((s8[8388608]{0:T(1024)(128)(4,1)}), s8[4194304]{0:T(1024)(128)(4,1)S(1)}, s32[]{:S(2)}) async-start(s8[8388608]{0:T(1024)(128)(4,1)} %bitcast.203), calls=%async_computation.4 | async-start | bytes 8388608
Sparse Core Ops, SparseCore 0:
  644.5 123.5 all-reduce.5
  771.4 86.2 all-reduce.7
where the time goes:
time: 926 us; the launch traced here: 915 us
  other arithmetic  284 us (31%)
  waiting for transfers between devices  207 us (22%)
  local copies, waits for them, and re-layouts  174 us (19%)
  matrix products  165 us (18%)
  blocking collectives  54.6 us (6%)
  between operations  16.2 us (2%)
    psum x2, waiting for transfers between devices, from_root(): return lax.psum(kept, axis)  201 us
    another operation x30, other arithmetic, factor_panel(): jnp.linalg.cholesky(cov_tile(panel_left, panel_right, decay_rate, nugget,...  173 us
    another operation x3, other arithmetic, factor_panel(): jax.scipy.linalg.solve_triangular(diag_factor, tiles.reshape(TR_DEV * B,...  83.5 us
    another operation x15, matrix products, factor_panel(): jax.scipy.linalg.solve_triangular(diag_factor, tiles.reshape(TR_DEV * B,...  77.4 us
    dot_general x6, matrix products, cov_tile(): jnp.einsum('...ka,kb->...ab', left, right, precision=lax.Precision.HIGHEST)  51.4 us
    scatter x1, local copies, waits for them, and re-layouts, body(): jnp.full((devices, capacity), -1, jnp.int32).at[home_dev, arrival_rank]  46.5 us
    unnamed x1, blocking collectives  38.2 us
    scatter x1, local copies, waits for them, and re-layouts, body(): row_home = jnp.full((TR_DEV, row_width), -1, jnp.int32).at[tile_index, go...  25.6 us
  transfers between devices with their start and end apart: 3, of which 3 were waited for; matrix products, arithmetic and copies ran while one was open for 0% of the time, Pallas kernels for 0%

commit v1 on v0

--- a/solution.py
+++ b/solution.py
@@ -11,7 +11,7 @@
 
 def from_root(value, axis, source):
     kept = jnp.where(lax.axis_index(axis) == source, value, 0).astype(value.dtype)
-    return lax.psum(kept, axis)
+    return jnp.sum(lax.all_gather(kept, axis), axis=0)
 
 
 def site_features(codes):

time: 926 us -> 1210 us (1.31)
  waiting for transfers between devices: 207 us -> 441 us
  other arithmetic: 284 us -> 322 us
    all_gather x0 -> x2, waiting for transfers between devices: none -> 435 us  [from_root(): return jnp.sum(lax.all_gather(kept, axis), axis=0)]
    psum x2 -> x0, waiting for transfers between devices: 201 us -> none  [from_root(): return lax.psum(kept, axis)]
    reduce_sum x0 -> x3, other arithmetic: none -> 32.6 us  [from_root(): return jnp.sum(lax.all_gather(kept, axis), axis=0)]
    all_gather x0 -> x1, blocking collectives: none -> 13.7 us  [from_root(): return jnp.sum(lax.all_gather(kept, axis), axis=0)]
where the time goes in v1:
time: 1210 us; the launch traced here: 1200 us
  waiting for transfers between devices  441 us (36%)
  other arithmetic  322 us (27%)
  local copies, waits for them, and re-layouts  185 us (15%)
  matrix products  165 us (14%)
  blocking collectives  59.9 us (5%)
  between operations  16 us (1%)
    all_gather x2, waiting for transfers between devices, from_root(): return jnp.sum(lax.all_gather(kept, axis), axis=0)  435 us
    another operation x30, other arithmetic, factor_panel(): jnp.linalg.cholesky(cov_tile(panel_left, panel_right, decay_rate, nugget,...  172 us
    another operation x3, other arithmetic, factor_panel(): jax.scipy.linalg.solve_triangular(diag_factor, tiles.reshape(TR_DEV * B,...  83.5 us
    another operation x15, matrix products, factor_panel(): jax.scipy.linalg.solve_triangular(diag_factor, tiles.reshape(TR_DEV * B,...  77.4 us
    dot_general x6, matrix products, cov_tile(): jnp.einsum('...ka,kb->...ab', left, right, precision=lax.Precision.HIGHEST)  51.3 us
    scatter x1, local copies, waits for them, and re-layouts, body(): jnp.full((devices, capacity), -1, jnp.int32).at[home_dev, arrival_rank]  46.5 us
    unnamed x1, blocking collectives  38.2 us
    reduce_sum x3, other arithmetic, from_root(): return jnp.sum(lax.all_gather(kept, axis), axis=0)  32.6 us
  transfers between devices with their start and end apart: 3, of which 3 were waited for; matrix products, arithmetic and copies ran while one was open for 0% of the time, Pallas kernels for 0%

profile of v1, /device:TPU:0, one launch (start us, length us, event | category | flops | bytes accessed | tf_op | source)
XLA Modules:
  0.0 1203.2 jit_solution(5827223571942501718)
XLA Ops:
  9.8 46.5 %scatter_fusion = s32[32,17]{0,1:T(8,128)S(1)} fusion(s32[32,17]{0,1:T(8,128)S(1)} %broadcast_in_dim.87, s32[544]{0:T(1024)S(1)} %fusion.112, s32[544]{0:T(1024)} %param.5), kind=kCustom, calls=%fused_computation | custom fusion | bytes 10880 | tf_op jit(solution)/shard_map/scatter | solution.py:57
  73.1 25.6 %scatter_fusion.1 = s32[4,128]{1,0:T(4,128)S(1)} fusion(s32[4,128]{1,0:T(4,128)S(1)} %broadcast_in_dim.89, s32[544]{0:T(1024)S(1)} %get-tuple-element.75, s32[544]{0:T(1024)S(1)} %reshape.1176), kind=kCustom, calls=%fused_computation.2 | custom fusion | bytes 10880 | tf_op jit(solution)/shard_map/scatter | solution.py:70
  111.4 38.2 %all-reduce.2 = s32[1024]{0:T(1024)S(1)} all-reduce(s32[1024]{0:T(1024)S(1)} %dynamic-update-slice.49), channel_id=1, replica_groups=mesh['prow'=4,'pcol'=8] {'prow','pcol'}, use_global_device_ids=true, to_apply=%add.2 | all-reduce | flops 1024 | bytes 8192
  150.1 485.5 %conditional.1 = (bf16[4,1024,1024]{2,1,0:T(8,128)(2,1)}) conditional(s32[]{:T(128)} %convert_element_type.130, () %tuple.14, (f32[]{:T(128)}, f32[4,1024]{1,0:T(4,128)S(1)}, f32[4,1024]{1,0:T(4,128)S(1)}, f32[]{:T(128)}, f32[4,4,1024]{2,0,1:T(4,128)S(1)}) %tuple.15), branch_computations={%region_6.7_spmd, %region_7.24_spmd} | conditional | flops 32137316352 | bytes 414441856 | solution.py:97
  173.7 11.7 cholesky.5
  185.5 9.8 custom-call.55
  201.7 11.9 cholesky.27
  216.1 9.8 custom-call.56
  229.3 11.7 cholesky.58
  242.9 9.8 custom-call.57
  256.7 11.7 cholesky.87
  270.3 9.8 custom-call.58
  283.6 11.7 cholesky.116
  297.2 10.0 custom-call.59
  310.5 11.7 cholesky.146
  324.1 9.8 custom-call.60
  336.9 12.1 %cholesky.176 = f32[128,128]{1,0:T(8,128)S(1)} custom-call(f32[128,128]{1,0:T(8,128)S(1)} %cholesky.256), custom_call_target="Cholesky" | custom-call | tf_op jit(solution)/shard_map/cond/branch_1_fun/jit(cholesky)/cholesky | solution.py:85
  351.0 9.8 custom-call.61
  363.4 11.7 cholesky.204
  381.9 23.2 %while.3 = (s32[]{:T(128)}, f32[1024,1024]{1,0:T(8,128)}, s32[8,2]{0,1:T(2,128)S(1)}, f32[8,128,128]{2,1,0:T(8,128)S(1)}, s32[]{:T(128)}) while((s32[]{:T(128)}, f32[1024,1024]{1,0:T(8,128)}, s32[8,2]{0,1:T(2,128)S(1)}, f32[8,128,128]{2,1,0:T(8,128)S(1)}, s32[]{:T(128)}) %tuple.98), condition=%wide.while_cond, body=%wide.while_body.sunk | while | flops 2 | bytes 131189 | solution.py:89
  405.2 78.6 %custom-call.62 = f32[8,128,128]{1,2,0:T(8,128)S(1)} custom-call(f32[8,128,128]{2,1,0:T(8,128)S(1)} %get-tuple-element.27), custom_call_target="InvertDiagBlocksLowerTriangular" | custom-call | tf_op jit(solution)/shard_map/cond/branch_1_fun/jit(_solve_triangular)/triangular_solve | solution.py:89
  483.8 23.3 %select_add_fusion = f32[4,1024,1024]{2,1,0:T(8,128)} fusion(f32[]{:T(128)S(6)} %mul.158, f32[]{:T(128)} %get-tuple-element.4, f32[4,4,1024]{2,0,1:T(4,128)S(1)} %get-tuple-element.71, f32[4,1024]{1,0:T(4,128)S(1)} %get-tuple-element.15), kind=kOutput, calls=%fused_computation.5 | convolution fusion | flops 234881024 | bytes 16859144 | tf_op jit(solution)/shard_map/cond/branch_1_fun/...ka,kb->...ab/dot_general | solution.py:28
  507.1 17.6 %copy.37 = f32[4096,1024]{0,1:T(8,128)} copy(f32[4096,1024]{1,0:T(8,128)} %bitcast.198) | data formatting | bytes 33554432 | tf_op jit(solution)/shard_map/cond/branch_1_fun/reshape | solution.py:90
  579.7 9.3 convolution_subtract_fusion.1
  594.5 9.9 convolution_subtract_fusion
  608.8 11.7 convolution_subtract_fusion.4
  623.4 11.9 copy.54
  643.0 300.1 %all-gather.7.cloned.1.call-done = bf16[32,1024,1024]{2,1,0:T(8,128)(2,1)} async-done(((bf16[4,1024,1024]{2,1,0:T(8,128)(2,1)}), bf16[32,1024,1024]{2,1,0:T(8,128)(2,1)}) %all-gather.7.cloned.1.call-update) | async-done | bytes 67108880 | tf_op jit(solution)/shard_map/all_gather | solution.py:14
  943.1 26.1 %reduce_sum.45 = bf16[4,1024,1024]{2,1,0:T(8,128)(2,1)} reduce(bf16[8,4,1024,1024]{3,2,1,0:T(8,128)(2,1)} %bitcast.33, bf16[]{:T(256)} %constant.564.clone.1), dimensions={0}, to_apply=%region_24.25 | reduce | flops 29360128 | bytes 75497472 | tf_op jit(solution)/shard_map/reduce_sum | solution.py:14
  987.7 10.6 copy.47
  999.2 13.7 %all-gather.3 = s32[4,1,1024]{2,1,0:T(1,128)S(1)} all-gather(s32[1,1,1024]{2,1,0:T(1,128)S(1)} %fusion.98), channel_id=3, replica_groups=mesh['prow'=4,'pcol'=8] {'prow'}, dimensions={0}, use_global_device_ids=true | all-gather | bytes 20480 | tf_op jit(solution)/shard_map/all_gather | solution.py:14
  1013.0 135.1 %all-gather.9.cloned.1.call-done = bf16[4,1024,1024]{2,1,0:T(8,128)(2,1)} async-done(((bf16[1,1024,1024]{2,1,0:T(8,128)(2,1)}), bf16[4,1024,1024]{2,1,0:T(8,128)(2,1)}) %all-gather.9.cloned.1.call-update) | async-done | bytes 8388624 | tf_op jit(solution)/shard_map/all_gather | solution.py:14
  (164 shorter events, 259.6 us)
Async XLA Ops:
  57.1 14.4 %all-to-all-start = ((s32[32,1,17]{2,1,0:T(1,128)}), s32[32,1,17]{2,1,0:T(1,128)S(1)}, u32[]{:S(2)}, u32[]{:S(2)}) async-start(s32[32,1,17]{2,1,0:T(1,128)} %copy.40), calls=%async_computation | async-start | bytes 32768 | tf_op jit(solution)/shard_map/all_to_all | solution.py:58
  64.4 878.7 %all-gather.7.cloned.1.call-start = ((), (), s32[]{:S(2)}) async-start(), calls=%async_computation.1 | async-start | bytes 75497472 | tf_op jit(solution)/shard_map/all_gather | solution.py:14
  154.3 1.9 copy-start.1
  171.7 2.0 copy-start.2
  524.7 11.9 copy-start
  642.9 505.1 %all-gather.9.cloned.1.call-start = ((), (), s32[]{:S(2)}) async-start(), calls=%async_computation.2 | async-start | bytes 10485760 | tf_op jit(solution)/shard_map/all_gather | solution.py:14
  1154.6 8.3 slice-start
  1158.7 4.1 slice-start.1
Sparse Core Ops, SparseCore 0:
  643.0 300.0 all-gather.6
  998.4 149.6 all-gather.8
